TPU v7x, 32 devices: a whole 2x2x4 slice. The times are simulated.
32 devices in a mesh: wshard: 4 (over y, x), ctx: 2 (over core), tp: 4 (over z).
Axes of the slice: x: 2, y: 2, z: 4, core: 2. Of those that a mesh axis runs over, the one named last changes fastest.
Arguments:
- tokens: bfloat16 [4, 2048, 768], P('wshard', 'ctx'), may hold values from -6 to 6
- lengths: int32 [4], P('wshard'), may hold values from 512 to 2048, as said below
- qkv_weight: bfloat16 [768, 3, 768], P('wshard', None, 'tp'), may hold values from -0.21875 to 0.21875
- qv_bias: float32 [2, 768], P(None, 'tp'), may hold values from -3 to 3
- out_weight: bfloat16 [768, 768], P('wshard', 'tp'), may hold values from -0.75 to 0.75
- out_bias: float32 [768], replicated, may hold values from -3 to 3
- ln1_gain: float32 [768], replicated, may hold values from 0.5 to 1.5
- ln1_bias: float32 [768], replicated, may hold values from -3 to 3
- gated_weight: bfloat16 [768, 2, 3072], P('wshard', None, 'tp'), may hold values from -0.21875 to 0.21875
- down_weight: bfloat16 [768, 3072], P('wshard', 'tp'), may hold values from -0.109375 to 0.109375
- down_bias: float32 [768], replicated, may hold values from -3 to 3
- ln2_gain: float32 [768], replicated, may hold values from 0.5 to 1.5
- ln2_bias: float32 [768], replicated, may hold values from -3 to 3
- cotangent: bfloat16 [4, 2048, 768], P('wshard', 'ctx'), may hold values from -6 to 6
Outputs:
- layer_output: bfloat16 [4, 2048, 768], P('wshard', 'ctx')
- input_grad: float32 [4, 2048, 768], P('wshard', 'ctx')
- qkv_grad: float32 [768, 3, 768], P('wshard', None, 'tp')
- qvbias_grad: float32 [2, 768], P(None, 'tp')
- outw_grad: float32 [768, 768], P('wshard', 'tp')
- outb_grad: float32 [768], replicated
- ln1g_grad: float32 [768], replicated
- ln1b_grad: float32 [768], replicated
- gated_grad: float32 [768, 2, 3072], P('wshard', None, 'tp')
- down_grad: float32 [768, 3072], P('wshard', 'tp')
- downb_grad: float32 [768], replicated
- ln2g_grad: float32 [768], replicated
- ln2b_grad: float32 [768], replicated
Inputs may be any that keep to these rules, and one draw needn't show every extreme that they name: Each sequence holds lengths[s] valid positions at its start; in every draw some sequence is full (2048) and some has exactly 512.
All inputs are finite; a program needn't handle non-finite values.
Results may differ from a plain program's by a relative error of at most 0.014.
The roundings to bfloat16 on the way count: a program that leaves them out, or rounds other values in their place, can miss the bound.
Values may be sent and summed in bfloat16 or wider, within the bound.
No kernel may reach another device: no remote copies, remote signals or barrier semaphores. Data moves between devices by JAX's collectives and lax.ppermute only.
A program may use at most 128 MiB of HBM per device.

v0:
```python
import jax
import jax.numpy as jnp
from jax import lax
from jax.sharding import PartitionSpec as P

HEADS = 12
DH = 64
norm_eps = 1e-05


def layer_norm(inputs, norm_gain, norm_shift):
    center = inputs - jnp.mean(inputs, axis=-1, keepdims=True)
    spread = jnp.mean(center * center, axis=-1, keepdims=True)
    return center * lax.rsqrt(spread + norm_eps) * norm_gain + norm_shift


def gated_unit(gate_part, up_part):
    return jax.nn.gelu(gate_part, approximate=False) * up_part


def times_transposed(left, right):
    return lax.dot_general(
        left, right, (((1,), (1,)), ((), ())), preferred_element_type=jnp.float32
    )


def first_transposed(left, right):
    return lax.dot_general(
        left, right, (((0,), (0,)), ((), ())), preferred_element_type=jnp.float32
    )


def alibi_scores(queries, key_block, length, query_start, slopes):
    raw_scores = jnp.einsum(
        "qhe,khe->hqk", queries, key_block, preferred_element_type=jnp.float32
    ) * DH ** (-0.5)
    query_pos = query_start + jnp.arange(queries.shape[0], dtype=jnp.int32)
    key_pos = jnp.arange(key_block.shape[0], dtype=jnp.int32)
    distance = jnp.abs(query_pos[:, None] - key_pos[None, :]).astype(jnp.float32)
    biased = raw_scores - slopes[:, None, None] * distance[None, :, :]
    return jnp.where((key_pos < length)[None, None, :], biased, -1e30)


def local(
    tokens,
    lengths,
    qkv_weight,
    qv_bias,
    out_weight,
    out_bias,
    ln1_gain,
    ln1_bias,
    gated_weight,
    down_weight,
    down_bias,
    ln2_gain,
    ln2_bias,
    cotangent,
):
    seq_dev, local_len, model_width = tokens.shape
    row_count = seq_dev * local_len
    part_width = qv_bias.shape[1]
    heads_local = part_width // DH
    ff_local = gated_weight.shape[2]
    shard_rows = qkv_weight.shape[0]
    tp_place = lax.axis_index("tp")
    query_start = lax.axis_index("ctx") * local_len
    head_number = tp_place * heads_local + jnp.arange(heads_local, dtype=jnp.int32) + 1
    slopes = 2.0 ** (-8.0 * head_number.astype(jnp.float32) / HEADS)
    full_qkv, full_out, full_gated, full_down = (
        lax.all_gather(qkv_weight, "wshard", axis=0, tiled=True),
        lax.all_gather(out_weight, "wshard", axis=0, tiled=True),
        lax.all_gather(gated_weight, "wshard", axis=0, tiled=True),
        lax.all_gather(down_weight, "wshard", axis=0, tiled=True),
    )
    token_rows = tokens.reshape(row_count, model_width)
    grad_rows = cotangent.reshape(row_count, model_width)
    projected = jnp.dot(
        token_rows,
        full_qkv.reshape(model_width, 3 * part_width),
        preferred_element_type=jnp.float32,
    ).reshape(row_count, 3, part_width)
    queries = (projected[:, 0] + qv_bias[0]).astype(jnp.bfloat16)
    keys_own = projected[:, 1].astype(jnp.bfloat16)
    values_own = (projected[:, 2] + qv_bias[1]).astype(jnp.bfloat16)
    keys_all, values_all = (
        lax.all_gather(keys_own.reshape(seq_dev, local_len, part_width), "ctx", axis=1, tiled=True),
        lax.all_gather(
            values_own.reshape(seq_dev, local_len, part_width), "ctx", axis=1, tiled=True
        ),
    )
    query_heads = queries.reshape(seq_dev, local_len, heads_local, DH)
    key_heads = keys_all.reshape(seq_dev, -1, heads_local, DH)
    value_heads = values_all.reshape(seq_dev, -1, heads_local, DH)

    def attend(entry):
        query_part, key_part, value_part, length = entry
        scores = alibi_scores(query_part, key_part, length, query_start, slopes)
        row_top = jnp.max(scores, axis=-1, keepdims=True)
        exponent = jnp.exp(scores - row_top)
        row_total = jnp.sum(exponent, axis=-1, keepdims=True)
        weights_low = (exponent / row_total).astype(jnp.bfloat16)
        mixture = jnp.einsum(
            "hqk,khe->qhe", weights_low, value_part, preferred_element_type=jnp.float32
        )
        return (mixture.astype(jnp.bfloat16), (row_top + jnp.log(row_total))[:, :, 0])

    mixture, log_total = lax.map(attend, (query_heads, key_heads, value_heads, lengths))
    mixed_rows = mixture.reshape(row_count, part_width)
    attn_part = times_transposed(mixed_rows, full_out)
    own_grads = grad_rows.astype(jnp.float32)
    pre_first = token_rows.astype(jnp.float32) + (lax.psum(attn_part, "tp") + out_bias)
    norm_first = layer_norm(pre_first, ln1_gain, ln1_bias)
    norm_low = norm_first.astype(jnp.bfloat16)
    gate_up = jnp.dot(
        norm_low, full_gated.reshape(model_width, 2 * ff_local), preferred_element_type=jnp.float32
    ).reshape(row_count, 2, ff_local)
    activation = gated_unit(gate_up[:, 0], gate_up[:, 1]).astype(jnp.bfloat16)
    down_part = times_transposed(activation, full_down)
    pre_second = norm_first + (lax.psum(down_part, "tp") + down_bias)
    layer_rows = layer_norm(pre_second, ln2_gain, ln2_bias)
    unused_second, pull_second = jax.vjp(layer_norm, pre_second, ln2_gain, ln2_bias)
    grad_pre2, gain_two, shift_two = pull_second(own_grads)
    output_low = layer_rows.astype(jnp.bfloat16)
    grad_down = grad_pre2.astype(jnp.bfloat16)
    grad_act = jnp.dot(grad_down, full_down, preferred_element_type=jnp.float32)
    unused_unit, pull_unit = jax.vjp(gated_unit, gate_up[:, 0], gate_up[:, 1])
    grad_gate, grad_up = pull_unit(grad_act)
    grad_gated = (
        jnp.stack([grad_gate, grad_up], axis=1)
        .astype(jnp.bfloat16)
        .reshape(row_count, 2 * ff_local)
    )
    back_part = times_transposed(grad_gated, full_gated.reshape(model_width, 2 * ff_local))
    grad_norm1 = grad_pre2 + lax.psum(back_part, "tp")
    unused_first, pull_first = jax.vjp(layer_norm, pre_first, ln1_gain, ln1_bias)
    grad_pre1, gain_one, shift_one = pull_first(grad_norm1)
    grad_attn = grad_pre1.astype(jnp.bfloat16)
    grad_mixed = jnp.dot(grad_attn, full_out, preferred_element_type=jnp.float32).astype(
        jnp.bfloat16
    )
    grad_heads = grad_mixed.reshape(seq_dev, local_len, heads_local, DH)

    def attend_back(entry):
        query_part, key_part, value_part, length, log_part, grad_part = entry
        scores = alibi_scores(query_part, key_part, length, query_start, slopes)
        attention = jnp.exp(scores - log_part[:, :, None])
        grad_weights = jnp.einsum(
            "qhe,khe->hqk", grad_part, value_part, preferred_element_type=jnp.float32
        )
        row_dot = jnp.sum(grad_weights * attention, axis=-1, keepdims=True)
        grad_scores = (attention * (grad_weights - row_dot)).astype(jnp.bfloat16)
        grad_query = jnp.einsum(
            "hqk,khe->qhe", grad_scores, key_part, preferred_element_type=jnp.float32
        ) * DH ** (-0.5)
        grad_key = jnp.einsum(
            "hqk,qhe->khe", grad_scores, query_part, preferred_element_type=jnp.float32
        ) * DH ** (-0.5)
        grad_value = jnp.einsum(
            "hqk,qhe->khe",
            attention.astype(jnp.bfloat16),
            grad_part,
            preferred_element_type=jnp.float32,
        )
        return (grad_query.astype(jnp.bfloat16), grad_key, grad_value)

    grad_query, grad_key_all, grad_value_all = lax.map(
        attend_back, (query_heads, key_heads, value_heads, lengths, log_total, grad_heads)
    )
    grad_key, grad_value = (
        lax.psum_scatter(
            grad_key_all.reshape(seq_dev, -1, part_width), "ctx", scatter_dimension=1, tiled=True
        ),
        lax.psum_scatter(
            grad_value_all.reshape(seq_dev, -1, part_width), "ctx", scatter_dimension=1, tiled=True
        ),
    )
    query_low = grad_query.reshape(row_count, part_width)
    value_low = grad_value.reshape(row_count, part_width).astype(jnp.bfloat16)
    grad_proj = jnp.stack(
        [query_low, grad_key.reshape(row_count, part_width).astype(jnp.bfloat16), value_low], axis=1
    ).reshape(row_count, 3 * part_width)
    input_part = times_transposed(grad_proj, full_qkv.reshape(model_width, 3 * part_width))
    input_rows = grad_pre1 + lax.psum(input_part, "tp")
    shard_grads = lax.psum_scatter(
        jnp.concatenate(
            [
                first_transposed(token_rows, grad_proj),
                first_transposed(grad_attn, mixed_rows),
                first_transposed(norm_low, grad_gated),
                first_transposed(grad_down, activation),
            ],
            axis=1,
        ),
        "wshard",
        scatter_dimension=0,
        tiled=True,
    )
    shard_grads = lax.psum(shard_grads, "ctx")
    qkv_end = 3 * part_width
    out_end = qkv_end + part_width
    gated_end = out_end + 2 * ff_local
    qkv_grad = shard_grads[:, :qkv_end].reshape(shard_rows, 3, part_width)
    outw_grad = shard_grads[:, qkv_end:out_end]
    gated_grad = shard_grads[:, out_end:gated_end].reshape(shard_rows, 2, ff_local)
    down_grad = shard_grads[:, gated_end:]
    bias_terms = jnp.stack(
        [
            jnp.sum(query_low.astype(jnp.float32), axis=0),
            jnp.sum(value_low.astype(jnp.float32), axis=0),
        ],
        axis=0,
    )
    qvbias_grad, outb_grad, ln1g_grad, ln1b_grad, downb_grad, ln2g_grad, ln2b_grad = lax.psum(
        (
            bias_terms,
            jnp.sum(grad_pre1, axis=0),
            gain_one,
            shift_one,
            jnp.sum(grad_pre2, axis=0),
            gain_two,
            shift_two,
        ),
        ("wshard", "ctx"),
    )
    layer_output = output_low.reshape(seq_dev, local_len, model_width)
    input_grad = input_rows.reshape(seq_dev, local_len, model_width)
    return (
        layer_output,
        input_grad,
        qkv_grad,
        qvbias_grad,
        outw_grad,
        outb_grad,
        ln1g_grad,
        ln1b_grad,
        gated_grad,
        down_grad,
        downb_grad,
        ln2g_grad,
        ln2b_grad,
    )


def solution(mesh):
    return jax.shard_map(
        local,
        mesh=mesh,
        in_specs=(
            P("wshard", "ctx", None),
            P("wshard"),
            P("wshard", None, "tp"),
            P(None, "tp"),
            P("wshard", "tp"),
            P(),
            P(),
            P(),
            P("wshard", None, "tp"),
            P("wshard", "tp"),
            P(),
            P(),
            P(),
            P("wshard", "ctx", None),
        ),
        out_specs=(
            P("wshard", "ctx", None),
            P("wshard", "ctx", None),
            P("wshard", None, "tp"),
            P(None, "tp"),
            P("wshard", "tp"),
            P(),
            P(),
            P(),
            P("wshard", None, "tp"),
            P("wshard", "tp"),
            P(),
            P(),
            P(),
        ),
        check_vma=False,
    )
```

profile of v0, /device:TPU:0, one launch (start us, length us, event | category | flops | bytes accessed | tf_op | source)
XLA Modules:
  0.0 759.2 jit_solution(12784075745873838943)
XLA Ops:
  8.1 17.1 %all_gather.18 = bf16[768,3,192]{2,0,1:T(8,128)(2,1)S(1)} all-gather(bf16[192,3,192]{2,0,1:T(8,128)(2,1)} %param.16), channel_id=1, replica_groups=mesh['wshard'=4,'ctx'=2,'tp'=4] {'wshard'}, dimensions={0}, use_global_device_ids=true | all-gather | bytes 1105920 | tf_op jit(solution)/shard_map/all_gather | solution.py:71
  25.2 1.3 copy.33
  26.6 2.3 fusion.37
  29.0 1.3 copy-done.19
  30.2 2.4 all-gather
  32.7 4.7 abs_convert_fusion
  38.1 1.2 fusion.48
  39.3 2.4 all_gather.19
  41.7 8.5 %all_gather.21 = bf16[768,192]{1,0:T(8,128)(2,1)S(1)} all-gather(bf16[192,192]{1,0:T(8,128)(2,1)S(1)} %copy-done.34), channel_id=1, replica_groups=mesh['wshard'=4,'ctx'=2,'tp'=4] {'wshard'}, dimensions={0}, use_global_device_ids=true | all-gather | bytes 368640 | tf_op jit(solution)/shard_map/all_gather | solution.py:72
  50.2 13.7 %fusion.62 = (f32[3,1024]{1,0:T(4,128)S(1)}, f32[3,1024,2048]{2,1,0:T(8,128)}) fusion(f32[1024,2048]{1,0:T(8,128)} %abs_convert_fusion, f32[3]{0:T(128)S(1)} %multiply_power_fusion, bf16[2048,3,64]{0,2,1:T(8,128)(2,1)S(1)} %bitcast.198, f32[1024,3,64]{0,2,1:T(8,128)S(1)} %bitcast.196, f32[3,64]{1,0:T(4,128)S(1)} %add.174, ...), kind=kOutput, calls=%fused_computation.121 | convolution fusion | flops 837153792 | bytes 35142412 | tf_op jit(solution)/shard_map/while/body/eval_jaxpr/qhe,khe->hqk/dot_general | solution.py:34
  63.9 10.4 %fusion = f32[3,1024]{1,0:T(4,128)S(1)} fusion(f32[3,1024,2048]{2,1,0:T(8,128)} %get-tuple-element.136, f32[3,1024]{1,0:T(4,128)S(1)} %get-tuple-element.135), kind=kLoop, calls=%fused_computation.6 | loop fusion | flops 12579840 | bytes 25190400 | tf_op jit(solution)/shard_map/while/body/eval_jaxpr/reduce_sum | solution.py:101
  74.4 10.6 %fusion.45 = bf16[3,64,1024]{2,1,0:T(8,128)(2,1)S(1)} fusion(bf16[2048,3,64]{0,2,1:T(8,128)(2,1)S(1)} %bitcast.206, f32[3,1024,2048]{2,1,0:T(8,128)} %get-tuple-element.136, f32[3,1024]{1,0:T(4,128)S(1)} %fusion, f32[3,1024]{1,0:T(4,128)S(1)} %get-tuple-element.135), kind=kOutput, calls=%fused_computation.85 | convolution fusion | flops 824377344 | bytes 26370048 | tf_op jit(solution)/shard_map/while/body/eval_jaxpr/hqk,khe->qhe/dot_general | solution.py:103
  85.0 0.7 copy-done.27
  85.7 2.3 fusion.63
  88.1 0.9 copy.34
  89.1 0.5 all-gather.6.cloned.1.call-update
  90.1 119.5 %all-reduce.7.cloned.1.call-done = f32[1024,768]{1,0:T(8,128)} async-done(((f32[1024,768]{1,0:T(8,128)}), f32[1024,768]{1,0:T(8,128)}) %all-reduce.7.cloned.1.call-update) | async-done | bytes 3145744 | tf_op jit(solution)/shard_map/psum | solution.py:112
  209.6 2.8 fusion.61
  213.0 4.3 copy.35
  217.3 4.6 fusion.33
  221.9 2.7 copy-done.11
  224.6 7.8 %multiply_convert_fusion.1 = (bf16[1024,768]{0,1:T(8,128)(2,1)}, f32[1024,768]{0,1:T(8,128)}) fusion(f32[1024,2,768]{0,2,1:T(8,128)S(1)} %fusion.33), kind=kLoop, calls=%fused_computation.46 | loop fusion | flops 51904512 | bytes 11010048 | tf_op jit(solution)/shard_map/convert_element_type | solution.py:118
  232.5 4.9 fusion.64
  237.6 120.0 %all-reduce.9.cloned.1.call-done = f32[1024,768]{1,0:T(8,128)} async-done(((f32[1024,768]{1,0:T(8,128)}), f32[1024,768]{1,0:T(8,128)}) %all-reduce.9.cloned.1.call-update) | async-done | bytes 3145744 | tf_op jit(solution)/shard_map/psum | solution.py:120
  357.6 2.9 fusion.59
  361.1 0.8 copy-done.6
  361.9 1.8 fusion.11
  363.7 2.6 fusion.58
  367.1 3.3 fusion.19
  370.5 1.1 copy-done.24
  372.1 4.4 convolution_bitcast_fusion.1
  376.8 119.9 %all-reduce.11.cloned.1.call-done = f32[1024,768]{1,0:T(8,128)} async-done(((f32[1024,768]{1,0:T(8,128)}), f32[1024,768]{1,0:T(8,128)}) %all-reduce.11.cloned.1.call-update) | async-done | bytes 3145744 | tf_op jit(solution)/shard_map/psum | solution.py:135
  496.8 4.4 multiply_reduce_fusion.1
  501.2 1.5 fusion.57
  502.7 1.6 copy-done.1
  504.3 0.8 convolution_convert_fusion
  505.1 16.4 %multiply_reduce_fusion = (f32[3,1024]{1,0:T(4,128)}, f32[3,1024,2048]{2,1,0:T(8,128)}) fusion(f32[3,1024,2048]{2,1,0:T(8,128)} %get-tuple-element.136, f32[3,1024]{1,0:T(4,128)S(1)} %log_add_fusion, bf16[1024,3,64]{0,2,1:T(8,128)(2,1)S(1)} %bitcast.203, bf16[2048,3,64]{0,2,1:T(8,128)(2,1)} %bitcast.207), kind=kOutput, calls=%fused_computation.1 | convolution fusion | flops 824177664 | bytes 51535872 | tf_op jit(solution)/shard_map/while/body/eval_jaxpr/qhe,khe->hqk/dot_general | solution.py:148
  521.5 17.0 %multiply_convert_fusion = bf16[3,1024,2048]{2,1,0:T(8,128)(2,1)S(1)} fusion(f32[3,1024,2048]{2,1,0:T(8,128)} %get-tuple-element.138, f32[3,1024,2048]{2,1,0:T(8,128)} %get-tuple-element.136, f32[3,1024]{1,0:T(4,128)} %get-tuple-element.137, f32[3,1024]{1,0:T(4,128)S(1)} %log_add_fusion), kind=kLoop, calls=%fused_computation | loop fusion | flops 25165824 | bytes 62939136 | tf_op jit(solution)/shard_map/while/body/eval_jaxpr/convert_element_type | solution.py:152
  538.6 4.0 convolution_multiply_fusion
  542.6 0.9 copy-done
  543.7 12.2 %fusion.2 = f32[3,64,2048]{2,1,0:T(8,128)} fusion(bf16[1024,3,64]{0,2,1:T(8,128)(2,1)S(1)} %bitcast.204, f32[3,1024,2048]{2,1,0:T(8,128)} %get-tuple-element.136, f32[3,1024]{1,0:T(4,128)S(1)} %log_add_fusion), kind=kOutput, calls=%fused_computation.8 | convolution fusion | flops 817889280 | bytes 27144192 | tf_op jit(solution)/shard_map/while/body/eval_jaxpr/hqk,qhe->khe/dot_general | solution.py:159
  556.2 2.3 maximum_convert_fusion
  559.6 3.1 fusion.51
  562.7 5.1 fusion.54
  567.8 0.8 fusion.53
  569.1 4.0 convert_reduce_fusion.2
  573.2 1.3 convert_bitcast_fusion.1
  574.5 1.3 convert_reduce_fusion.1
  575.9 0.6 copy-done.20
  576.5 2.3 fusion.41
  578.8 1.9 copy.37
  580.7 9.9 %concatenate.3 = f32[768,3072]{1,0:T(8,128)} concatenate(f32[768,576]{1,0:T(8,128)S(1)} %copy.37, f32[768,192]{1,0:T(8,128)S(1)} %fusion.53, f32[768,1536]{1,0:T(8,128)} %fusion.54, f32[768,768]{1,0:T(8,128)} %fusion.51), dimensions={1} | concatenate | bytes 18874368 | tf_op jit(solution)/shard_map/concatenate | solution.py:186
  590.7 1.2 copy-done.13
  592.0 3.1 convolution_bitcast_fusion
  595.2 89.0 %reduce-scatter.8.cloned.1.call-done = f32[192,3072]{1,0:T(8,128)} async-done(((f32[768,3072]{1,0:T(8,128)}), f32[192,3072]{1,0:T(8,128)}) %reduce-scatter.8.cloned.1.call-update) | async-done | bytes 2359312 | tf_op jit(solution)/shard_map/reduce_scatter | solution.py:185
  684.3 1.7 convert_reduce_fusion
  686.1 28.9 %all-reduce.13.cloned.1.call-done = f32[1024,768]{1,0:T(8,128)} async-done(((f32[1024,768]{1,0:T(8,128)}), f32[1024,768]{1,0:T(8,128)}) %all-reduce.13.cloned.1.call-update) | async-done | bytes 3145744 | tf_op jit(solution)/shard_map/psum | solution.py:184
  715.0 4.0 add_reduce_fusion
  719.0 24.4 %all-reduce = (f32[2,192]{1,0:T(2,128)}, f32[768]{0:T(1024)}, f32[768]{0:T(1024)}, f32[768]{0:T(1024)}, f32[768]{0:T(1024)}, /*index=5*/f32[768]{0:T(1024)}, f32[768]{0:T(1024)}) all-reduce(f32[2,192]{1,0:T(2,128)S(1)} %pad_maximum_fusion.1, ...), channel_id=1, replica_groups=mesh['wshard'=4,'ctx'=2,'tp'=4] {'wshard','ctx'}, use_global_device_ids=true, to_apply=%region_21.22 | all-reduce | flops 4992 | bytes 39936 | tf_op jit(solution)/shard_map/psum | solution.py:214
  743.4 1.3 slice-done.5
  744.7 1.8 reshape.302
  746.7 1.1 copy.41
  747.7 1.9 slice.55
  749.7 1.8 slice.53
  (162 shorter events, 6.5 us)
Async XLA Ops:
  8.0 18.5 %copy-start.22 = (bf16[1,1024,768]{2,1,0:T(8,128)(2,1)S(1)}, bf16[1,1024,768]{2,1,0:T(8,128)(2,1)}, u32[]{:S(2)}) copy-start(bf16[1,1024,768]{2,1,0:T(8,128)(2,1)} %param.14) | copy-start | bytes 4718596
  8.0 201.6 %all-reduce.7.cloned.1.call-start = ((), (), s32[]{:S(2)}) async-start(), calls=%async_computation.3 | async-start | bytes 6291456 | tf_op jit(solution)/shard_map/psum | solution.py:112
  25.2 3.6 copy-start.12
  28.8 1.4 copy-start.19
  28.9 3.8 copy-start.53
  30.2 19.9 %copy-start.4 = (f32[1024,1,192]{0,2,1:T(8,128)}, f32[1024,1,192]{0,2,1:T(8,128)S(1)}, u32[]{:S(2)}) copy-start(f32[1024,1,192]{0,2,1:T(8,128)S(1)} %slice.48) | copy-start | bytes 2359300
  32.6 17.6 %copy-start.9 = (bf16[2048,1,192]{0,2,1:T(8,128)(2,1)}, bf16[2048,1,192]{0,2,1:T(8,128)(2,1)S(1)}, u32[]{:S(2)}) copy-start(bf16[2048,1,192]{0,2,1:T(8,128)(2,1)S(1)} %all-gather) | copy-start | bytes 2359300
  32.7 17.5 %copy-start.32 = (f32[3,64]{1,0:T(4,128)}, f32[3,64]{1,0:T(4,128)S(1)}, u32[]{:S(2)}) copy-start(f32[3,64]{1,0:T(4,128)S(1)} %add.174) | copy-start | bytes 2308
  32.7 9.0 %copy-start.34 = (bf16[192,192]{1,0:T(8,128)(2,1)S(1)}, bf16[192,192]{1,0:T(8,128)(2,1)}, u32[]{:S(2)}) copy-start(bf16[192,192]{1,0:T(8,128)(2,1)} %param.18) | copy-start | bytes 221188
  41.7 32.7 %copy-start.17 = (bf16[1,2048,192]{1,2,0:T(8,128)(2,1)}, bf16[1,2048,192]{1,2,0:T(8,128)(2,1)S(1)}, u32[]{:S(2)}) copy-start(bf16[1,2048,192]{1,2,0:T(8,128)(2,1)S(1)} %all_gather.19) | copy-start | bytes 2359300
  50.2 34.8 %copy-start.14 = (bf16[768,192]{1,0:T(8,128)(2,1)}, bf16[768,192]{1,0:T(8,128)(2,1)S(1)}, u32[]{:S(2)}) copy-start(bf16[768,192]{1,0:T(8,128)(2,1)S(1)} %all_gather.21) | copy-start | bytes 884740
  85.7 2.4 copy-start.29
  88.0 121.6 %copy-start.48 = (f32[768]{0:T(1024)S(1)}, f32[768]{0:T(1024)}, u32[]{:S(2)}) copy-start(f32[768]{0:T(1024)} %param.19) | copy-start | bytes 9220
  88.1 124.9 %all-gather.4.cloned.1.call-start = ((), (), s32[]{:S(2)}) async-start(), calls=%async_computation.4 | async-start | bytes 2949120 | tf_op jit(solution)/shard_map/all_gather | solution.py:73
  89.0 143.4 %all-gather.6.cloned.1.call-start = ((), (), s32[]{:S(2)}) async-start(), calls=%async_computation.5 | async-start | bytes 1474560 | tf_op jit(solution)/shard_map/all_gather | solution.py:74
  89.6 268.0 %all-reduce.9.cloned.1.call-start = ((), (), s32[]{:S(2)}) async-start(), calls=%async_computation.6 | async-start | bytes 6291456 | tf_op jit(solution)/shard_map/psum | solution.py:120
  212.4 288.7 %copy-start.30 = (f32[1024]{0:T(1024)}, f32[1024]{0:T(1024)S(1)}, u32[]{:S(2)}) copy-start(f32[1024]{0:T(1024)S(1)} %broadcast_multiply_fusion.1) | copy-start | bytes 12292
  212.9 4.4 copy-start.39
  212.9 4.3 copy-start.51
  213.0 288.2 %copy-start.35 = (f32[1024]{0:T(1024)}, f32[1024]{0:T(1024)S(1)}, u32[]{:S(2)}) copy-start(f32[1024]{0:T(1024)S(1)} %fusion.49) | copy-start | bytes 12292
  221.9 2.7 copy-start.11
  237.4 120.2 %copy-start.49 = (f32[768]{0:T(1024)S(1)}, f32[768]{0:T(1024)}, u32[]{:S(2)}) copy-start(f32[768]{0:T(1024)} %param.24) | copy-start | bytes 9220
  237.4 259.4 %all-reduce.11.cloned.1.call-start = ((), (), s32[]{:S(2)}) async-start(), calls=%async_computation.7 | async-start | bytes 6291456 | tf_op jit(solution)/shard_map/psum | solution.py:135
  360.5 1.4 copy-start.6
  361.0 2.7 copy-start.50
  361.9 4.4 slice-start.3
  363.7 2.6 slice-start.4
  363.7 2.9 copy-start.16
  363.7 3.4 copy-start.54
  366.3 4.2 copy-start.7
  366.3 130.4 %copy-start.41 = (f32[1024]{0:T(1024)}, f32[1024]{0:T(1024)S(1)}, u32[]{:S(2)}) copy-start(f32[1024]{0:T(1024)S(1)} %negate_multiply_fusion.2) | copy-start | bytes 12292
  367.1 5.0 copy-start.18
  370.5 1.6 copy-start.25
  376.5 196.6 %reduce-scatter.4.cloned.1.call-start = ((), (), s32[]{:S(2)}) async-start(), calls=%async_computation.8 | async-start | bytes 2359296 | tf_op jit(solution)/shard_map/reduce_scatter | solution.py:171
  501.1 3.1 copy-start.15
  502.6 1.7 copy-start.1
  502.6 2.5 copy-start.37
  521.5 17.0 %copy-start.5 = (f32[1024,1,192]{0,2,1:T(8,128)S(1)}, f32[1024,1,192]{0,2,1:T(8,128)}, u32[]{:S(2)}) copy-start(f32[1024,1,192]{0,2,1:T(8,128)} %copy-done.4) | copy-start | bytes 2359300
  521.5 17.1 %copy-start.33 = (f32[3,64]{1,0:T(4,128)S(1)}, f32[3,64]{1,0:T(4,128)}, u32[]{:S(2)}) copy-start(f32[3,64]{1,0:T(4,128)} %copy-done.32) | copy-start | bytes 2308
  538.6 5.0 copy-start
  543.6 30.9 %reduce-scatter.6.cloned.1.call-start = ((), (), s32[]{:S(2)}) async-start(), calls=%async_computation.9 | async-start | bytes 2359296 | tf_op jit(solution)/shard_map/reduce_scatter | solution.py:174
  555.9 2.7 copy-start.42
  555.9 128.3 %reduce-scatter.8.cloned.1.call-start = ((), (), s32[]{:S(2)}) async-start(), calls=%async_computation.11 | async-start | bytes 11796480 | tf_op jit(solution)/shard_map/reduce_scatter | solution.py:185
  556.2 2.8 copy-start.8
  556.2 3.3 copy-start.26
  559.5 3.1 copy-start.31
  559.5 3.1 copy-start.36
  559.5 3.1 copy-start.40
  559.5 3.1 copy-start.52
  559.5 9.1 %slice-start = ((s8[12582912]{0:T(1024)(128)(4,1)}), s8[4194304]{0:T(1024)(128)(4,1)S(1)}, s32[]{:S(2)}) async-start(s8[12582912]{0:T(1024)(128)(4,1)} %bitcast.193), calls=%async_computation.13 | async-start | bytes 8388608
  559.5 9.1 %slice-start.1 = ((s8[12582912]{0:T(1024)(128)(4,1)}), s8[4194304]{0:T(1024)(128)(4,1)S(1)}, s32[]{:S(2)}) async-start(s8[12582912]{0:T(1024)(128)(4,1)} %bitcast.193), calls=%async_computation.14 | async-start | bytes 8388608
  562.6 5.1 copy-start.2
  562.6 5.1 copy-start.28
  562.6 5.1 copy-start.38
  562.7 6.0 slice-start.2
  573.1 3.4 copy-start.23
  590.7 124.3 %all-reduce.13.cloned.1.call-start = ((), (), s32[]{:S(2)}) async-start(), calls=%async_computation.10 | async-start | bytes 6291456 | tf_op jit(solution)/shard_map/psum | solution.py:184
  595.1 119.9 %copy-start.3 = (f32[1024,768]{1,0:T(8,128)S(1)}, f32[1024,768]{1,0:T(8,128)}, u32[]{:S(2)}) copy-start(f32[1024,768]{1,0:T(8,128)} %copy-done.1) | copy-start | bytes 9437188
  595.1 148.2 %all-reduce.15.cloned.1.call-start = ((), (), s32[]{:S(2)}) async-start(), calls=%async_computation.12 | async-start | bytes 4718592 | tf_op jit(solution)/shard_map/psum | solution.py:199
  686.0 32.9 %copy-start.43 = (f32[768]{0:T(1024)S(1)}, f32[768]{0:T(1024)}, u32[]{:S(2)}) copy-start(f32[768]{0:T(1024)} %get-tuple-element.102) | copy-start | bytes 9220
  686.0 32.9 %copy-start.44 = (f32[768]{0:T(1024)S(1)}, f32[768]{0:T(1024)}, u32[]{:S(2)}) copy-start(f32[768]{0:T(1024)} %get-tuple-element.106) | copy-start | bytes 9220
  686.1 32.9 %copy-start.45 = (f32[768]{0:T(1024)S(1)}, f32[768]{0:T(1024)}, u32[]{:S(2)}) copy-start(f32[768]{0:T(1024)} %get-tuple-element.128) | copy-start | bytes 9220
  686.1 32.9 %copy-start.47 = (f32[768]{0:T(1024)S(1)}, f32[768]{0:T(1024)}, u32[]{:S(2)}) copy-start(f32[768]{0:T(1024)} %get-tuple-element.104) | copy-start | bytes 9220
  743.4 3.1 slice-start.6
  (8 other events, 9.3 us)
Sparse Core Ops, SparseCore 0:
  88.2 121.3 all-reduce.6
  237.5 120.0 all-reduce.8
  376.7 120.0 all-reduce.10
  595.3 119.6 all-reduce.12
  717.2 20.7 all-reduce.14
Sparse Core Ops, SparseCore 1:
  91.0 37.5 all-gather.3
  130.2 27.4 all-gather.5
  543.7 7.8 reduce-scatter.3
  556.0 8.0 reduce-scatter.5
  590.8 93.4 reduce-scatter.7
where the time goes:
time: 768 us; the launch traced here: 759 us
  waiting for transfers between devices  478 us (62%)
  matrix products  98.1 us (13%)
  other arithmetic  68.9 us (9%)
  blocking collectives  54.8 us (7%)
  local copies, waits for them, and re-layouts  40.6 us (5%)
  between operations  17.3 us (2%)
    psum x1, waiting for transfers between devices, local(): pre_second = norm_first + (lax.psum(down_part, 'tp') + down_bias)  120 us
    psum x1, waiting for transfers between devices, local(): grad_norm1 = grad_pre2 + lax.psum(back_part, 'tp')  120 us
    psum x1, waiting for transfers between devices, local(): lax.psum(attn_part, 'tp') + out_bias  119 us
    reduce_scatter x1, waiting for transfers between devices, local(): lax.psum_scatter(jnp.concatenate([first_transposed(token_rows, grad_proj)...  89 us
    psum x1, waiting for transfers between devices, local(): input_rows = grad_pre1 + lax.psum(input_part, 'tp')  28.9 us
    psum x1, blocking collectives, local(): lax.psum((bias_terms, jnp.sum(grad_pre1, axis=0), gain_one, shift_one, jn...  24.4 us
    all_gather x1, blocking collectives, local(): lax.all_gather(qkv_weight, 'wshard', axis=0, tiled=True)  17.1 us
    convert_element_type x1, other arithmetic, attend_back(): grad_scores = (attention * (grad_weights - row_dot)).astype(jnp.bfloat16)  17 us
  transfers between devices with their start and end apart: 10, of which 5 were waited for; matrix products, arithmetic and copies ran while one was open for 8% of the time, Pallas kernels for 0%

commit v1 on v0

--- a/solution.py
+++ b/solution.py
@@ -6,6 +6,10 @@
 HEADS = 12
 DH = 64
 norm_eps = 1e-05
+
+
+def view_stops_all_up(local_block):
+    return jnp.sum(lax.all_gather(local_block, "tp"), axis=0)
 
 
 def layer_norm(inputs, norm_gain, norm_shift):
@@ -109,7 +113,7 @@
     mixed_rows = mixture.reshape(row_count, part_width)
     attn_part = times_transposed(mixed_rows, full_out)
     own_grads = grad_rows.astype(jnp.float32)
-    pre_first = token_rows.astype(jnp.float32) + (lax.psum(attn_part, "tp") + out_bias)
+    pre_first = token_rows.astype(jnp.float32) + (view_stops_all_up(attn_part) + out_bias)
     norm_first = layer_norm(pre_first, ln1_gain, ln1_bias)
     norm_low = norm_first.astype(jnp.bfloat16)
     gate_up = jnp.dot(

time: 768 us -> 978 us (1.27)
  waiting for transfers between devices: 478 us -> 665 us
  other arithmetic: 68.9 us -> 80.2 us
    all_gather x0 -> x1, waiting for transfers between devices: none -> 213 us  [view_stops_all_up(): return jnp.sum(lax.all_gather(local_block, 'tp'), axis=0)]
    psum x1 -> x0, waiting for transfers between devices: 119 us -> none  [local(): lax.psum(attn_part, 'tp') + out_bias]
    psum x1, waiting for transfers between devices: 28.9 us -> 122 us  [local(): input_rows = grad_pre1 + lax.psum(input_part, 'tp')]
  transfers between devices with their start and end apart: 10 -> 10, of which waited for: 5 -> 6; matrix products, arithmetic and copies ran while one was open for 8% -> 12% of each run, Pallas kernels for 0% -> 0%
where the time goes in v1:
time: 978 us; the launch traced here: 969 us
  waiting for transfers between devices  665 us (68%)
  matrix products  102 us (10%)
  other arithmetic  80.2 us (8%)
  blocking collectives  60.9 us (6%)
  local copies, waits for them, and re-layouts  43.6 us (4%)
  between operations  15.9 us (2%)
    all_gather x1, waiting for transfers between devices, view_stops_all_up(): return jnp.sum(lax.all_gather(local_block, 'tp'), axis=0)  213 us
    psum x1, waiting for transfers between devices, local(): input_rows = grad_pre1 + lax.psum(input_part, 'tp')  122 us
    psum x1, waiting for transfers between devices, local(): pre_second = norm_first + (lax.psum(down_part, 'tp') + down_bias)  121 us
    psum x1, waiting for transfers between devices, local(): grad_norm1 = grad_pre2 + lax.psum(back_part, 'tp')  119 us
    reduce_scatter x1, waiting for transfers between devices, local(): lax.psum_scatter(jnp.concatenate([first_transposed(token_rows, grad_proj)...  88.6 us
    psum x1, blocking collectives, local(): lax.psum((bias_terms, jnp.sum(grad_pre1, axis=0), gain_one, shift_one, jn...  24.4 us
    all_gather x1, blocking collectives, local(): lax.all_gather(qkv_weight, 'wshard', axis=0, tiled=True)  21.4 us
  transfers between devices with their start and end apart: 10, of which 6 were waited for; matrix products, arithmetic and copies ran while one was open for 12% of the time, Pallas kernels for 0%

profile of v1, /device:TPU:0, one launch (start us, length us, event | category | flops | bytes accessed | tf_op | source)
XLA Modules:
  0.0 969.2 jit_solution(9248503156232428800)
XLA Ops:
  7.2 2.0 copy.34
  9.4 21.4 %all_gather.24 = bf16[768,3,192]{2,0,1:T(8,128)(2,1)S(1)} all-gather(bf16[192,3,192]{2,0,1:T(8,128)(2,1)} %param.16), channel_id=1, replica_groups=mesh['wshard'=4,'ctx'=2,'tp'=4] {'wshard'}, dimensions={0}, use_global_device_ids=true | all-gather | bytes 1105920 | tf_op jit(solution)/shard_map/all_gather | solution.py:75
  30.8 1.3 copy.33
  32.1 2.3 fusion.45
  34.5 1.3 copy-done.20
  35.8 2.4 all-gather
  38.3 4.7 abs_convert_fusion
  43.6 1.2 fusion.57
  44.8 2.4 all_gather.25
  47.2 10.3 %all_gather.27 = bf16[768,192]{1,0:T(8,128)(2,1)S(1)} all-gather(bf16[192,192]{1,0:T(8,128)(2,1)S(1)} %copy-done.36), channel_id=1, replica_groups=mesh['wshard'=4,'ctx'=2,'tp'=4] {'wshard'}, dimensions={0}, use_global_device_ids=true | all-gather | bytes 368640 | tf_op jit(solution)/shard_map/all_gather | solution.py:76
  57.6 13.6 %fusion.68 = (f32[3,1024]{1,0:T(4,128)S(1)}, f32[3,1024,2048]{2,1,0:T(8,128)}) fusion(f32[1024,2048]{1,0:T(8,128)} %abs_convert_fusion, f32[3]{0:T(128)S(1)} %multiply_power_fusion, bf16[2048,3,64]{0,2,1:T(8,128)(2,1)S(1)} %bitcast.223, f32[1024,3,64]{0,2,1:T(8,128)S(1)} %bitcast.220, f32[3,64]{1,0:T(4,128)S(1)} %add.194, ...), kind=kOutput, calls=%fused_computation.129 | convolution fusion | flops 837153792 | bytes 35142412 | tf_op jit(solution)/shard_map/while/body/eval_jaxpr/qhe,khe->hqk/dot_general | solution.py:38
  71.2 10.4 %fusion = f32[3,1024]{1,0:T(4,128)S(1)} fusion(f32[3,1024,2048]{2,1,0:T(8,128)} %get-tuple-element.136, f32[3,1024]{1,0:T(4,128)S(1)} %get-tuple-element.135), kind=kLoop, calls=%fused_computation.6 | loop fusion | flops 12579840 | bytes 25190400 | tf_op jit(solution)/shard_map/while/body/eval_jaxpr/reduce_sum | solution.py:105
  81.7 10.6 %fusion.54 = bf16[3,64,1024]{2,1,0:T(8,128)(2,1)S(1)} fusion(bf16[2048,3,64]{0,2,1:T(8,128)(2,1)S(1)} %bitcast.231, f32[3,1024,2048]{2,1,0:T(8,128)} %get-tuple-element.136, f32[3,1024]{1,0:T(4,128)S(1)} %fusion, f32[3,1024]{1,0:T(4,128)S(1)} %get-tuple-element.135), kind=kOutput, calls=%fused_computation.94 | convolution fusion | flops 824377344 | bytes 26370048 | tf_op jit(solution)/shard_map/while/body/eval_jaxpr/hqk,khe->qhe/dot_general | solution.py:107
  92.3 2.3 fusion.69
  95.9 4.3 copy.35
  100.2 213.0 %all-gather.10.cloned.1.call-done = f32[4096,768]{1,0:T(8,128)} async-done(((f32[1024,768]{1,0:T(8,128)}), f32[4096,768]{1,0:T(8,128)}) %all-gather.10.cloned.1.call-update) | async-done | bytes 12582928 | tf_op jit(solution)/shard_map/all_gather | solution.py:12
  313.2 7.5 reduce_sum.176
  320.7 3.0 fusion.67
  325.6 0.8 fusion.25
  326.4 0.9 copy-done.19
  327.3 2.8 fusion.38
  330.1 2.7 copy-done.10
  332.8 7.9 multiply_convert_fusion.2
  340.9 4.9 fusion.70
  346.0 121.0 %all-reduce.6.cloned.1.call-done = f32[1024,768]{1,0:T(8,128)} async-done(((f32[1024,768]{1,0:T(8,128)}), f32[1024,768]{1,0:T(8,128)}) %all-reduce.6.cloned.1.call-update) | async-done | bytes 3145744 | tf_op jit(solution)/shard_map/psum | solution.py:124
  467.0 2.9 fusion.65
  470.5 0.8 copy-done.6
  471.3 1.8 fusion.11
  473.1 2.6 fusion.64
  476.6 3.4 fusion.49
  480.0 1.1 copy-done.24
  481.6 4.4 convolution_bitcast_fusion.1
  487.0 119.2 %all-reduce.8.cloned.1.call-done = f32[1024,768]{1,0:T(8,128)} async-done(((f32[1024,768]{1,0:T(8,128)}), f32[1024,768]{1,0:T(8,128)}) %all-reduce.8.cloned.1.call-update) | async-done | bytes 3145744 | tf_op jit(solution)/shard_map/psum | solution.py:139
  606.2 4.9 multiply_reduce_fusion.1
  611.2 1.5 fusion.63
  612.7 1.6 copy-done.1
  614.3 0.8 convolution_convert_fusion
  615.2 19.4 %multiply_reduce_fusion = (f32[3,1024]{1,0:T(4,128)S(1)}, f32[3,1024,2048]{2,1,0:T(8,128)}) fusion(f32[3,1024,2048]{2,1,0:T(8,128)} %get-tuple-element.136, f32[3,1024]{1,0:T(4,128)S(1)} %log_add_fusion, bf16[1024,3,64]{0,2,1:T(8,128)(2,1)S(1)} %bitcast.228, bf16[2048,3,64]{0,2,1:T(8,128)(2,1)S(1)} %bitcast.232), kind=kOutput, calls=%fused_computation.1 | convolution fusion | flops 824177664 | bytes 51535872 | tf_op jit(solution)/shard_map/while/body/eval_jaxpr/qhe,khe->hqk/dot_general | solution.py:152
  634.6 16.8 %multiply_convert_fusion = bf16[3,1024,2048]{2,1,0:T(8,128)(2,1)S(1)} fusion(f32[3,1024,2048]{2,1,0:T(8,128)} %get-tuple-element.138, f32[3,1024,2048]{2,1,0:T(8,128)} %get-tuple-element.136, f32[3,1024]{1,0:T(4,128)S(1)} %get-tuple-element.137, f32[3,1024]{1,0:T(4,128)S(1)} %log_add_fusion), kind=kLoop, calls=%fused_computation | loop fusion | flops 25165824 | bytes 62939136 | tf_op jit(solution)/shard_map/while/body/eval_jaxpr/convert_element_type | solution.py:156
  651.4 4.1 convolution_multiply_fusion
  655.5 0.9 copy-done
  656.5 12.2 %fusion.2 = f32[3,64,2048]{2,1,0:T(8,128)} fusion(bf16[1024,3,64]{0,2,1:T(8,128)(2,1)S(1)} %bitcast.229, f32[3,1024,2048]{2,1,0:T(8,128)} %get-tuple-element.136, f32[3,1024]{1,0:T(4,128)S(1)} %log_add_fusion), kind=kOutput, calls=%fused_computation.8 | convolution fusion | flops 817889280 | bytes 27144192 | tf_op jit(solution)/shard_map/while/body/eval_jaxpr/hqk,qhe->khe/dot_general | solution.py:163
  669.1 2.3 pad_maximum_fusion
  672.1 3.0 fusion.60
  675.2 4.4 fusion.43
  679.6 1.7 fusion.62
  681.8 5.2 convert_reduce_fusion.2
  687.0 1.9 convert_bitcast_fusion.1
  688.9 1.4 convert_reduce_fusion.1
  691.0 1.1 pad_maximum_fusion.1
  692.2 2.3 fusion.50
  694.5 2.8 copy.37
  697.3 10.7 %concatenate.3 = f32[768,3072]{1,0:T(8,128)} concatenate(f32[768,576]{1,0:T(8,128)} %copy.37, f32[768,192]{1,0:T(8,128)} %fusion.62, f32[768,1536]{1,0:T(8,128)} %fusion.43, f32[768,768]{1,0:T(8,128)} %fusion.60), dimensions={1} | concatenate | bytes 18874368 | tf_op jit(solution)/shard_map/concatenate | solution.py:190
  708.1 4.7 convolution_bitcast_fusion
  712.8 88.6 %reduce-scatter.8.cloned.1.call-done = f32[192,3072]{1,0:T(8,128)} async-done(((f32[768,3072]{1,0:T(8,128)}), f32[192,3072]{1,0:T(8,128)}) %reduce-scatter.8.cloned.1.call-update) | async-done | bytes 2359312 | tf_op jit(solution)/shard_map/reduce_scatter | solution.py:189
  801.5 1.7 convert_reduce_fusion
  803.3 122.2 %all-reduce.10.cloned.1.call-done = f32[1024,768]{1,0:T(8,128)} async-done(((f32[1024,768]{1,0:T(8,128)}), f32[1024,768]{1,0:T(8,128)}) %all-reduce.10.cloned.1.call-update) | async-done | bytes 3145744 | tf_op jit(solution)/shard_map/psum | solution.py:188
  925.5 4.0 add_reduce_fusion
  929.5 24.4 %all-reduce = (f32[2,192]{1,0:T(2,128)}, f32[768]{0:T(1024)}, f32[768]{0:T(1024)}, f32[768]{0:T(1024)}, f32[768]{0:T(1024)}, /*index=5*/f32[768]{0:T(1024)}, f32[768]{0:T(1024)}) all-reduce(f32[2,192]{1,0:T(2,128)S(1)} %pad_maximum_fusion.2, ...), channel_id=1, replica_groups=mesh['wshard'=4,'ctx'=2,'tp'=4] {'wshard','ctx'}, use_global_device_ids=true, to_apply=%region_21.22 | all-reduce | flops 4992 | bytes 39936 | tf_op jit(solution)/shard_map/psum | solution.py:218
  953.9 1.3 slice-done.5
  955.2 1.8 reshape.391
  957.2 1.1 copy.41
  958.3 1.9 slice.55
  960.2 1.8 slice.53
  (168 shorter events, 9.7 us)
Async XLA Ops:
  7.2 24.9 %copy-start.11 = (bf16[1,1024,768]{2,1,0:T(8,128)(2,1)S(1)}, bf16[1,1024,768]{2,1,0:T(8,128)(2,1)}, u32[]{:S(2)}) copy-start(bf16[1,1024,768]{2,1,0:T(8,128)(2,1)} %param.14) | copy-start | bytes 4718596
  7.2 88.7 %all-gather.6.cloned.1.call-start = ((), (), s32[]{:S(2)}) async-start(), calls=%async_computation.3 | async-start | bytes 2949120 | tf_op jit(solution)/shard_map/all_gather | solution.py:77
  9.3 303.9 %all-gather.10.cloned.1.call-start = ((), (), s32[]{:S(2)}) async-start(), calls=%async_computation.12 | async-start | bytes 15728640 | tf_op jit(solution)/shard_map/all_gather | solution.py:12
  30.8 3.6 copy-start.14
  34.4 3.8 copy-start.55
  35.8 21.8 %copy-start.4 = (f32[1024,1,192]{0,2,1:T(8,128)}, f32[1024,1,192]{0,2,1:T(8,128)S(1)}, u32[]{:S(2)}) copy-start(f32[1024,1,192]{0,2,1:T(8,128)S(1)} %slice.48) | copy-start | bytes 2359300
  38.1 19.4 %copy-start.9 = (bf16[2048,1,192]{0,2,1:T(8,128)(2,1)}, bf16[2048,1,192]{0,2,1:T(8,128)(2,1)S(1)}, u32[]{:S(2)}) copy-start(bf16[2048,1,192]{0,2,1:T(8,128)(2,1)S(1)} %all-gather) | copy-start | bytes 2359300
  38.2 19.3 %copy-start.34 = (f32[3,64]{1,0:T(4,128)}, f32[3,64]{1,0:T(4,128)S(1)}, u32[]{:S(2)}) copy-start(f32[3,64]{1,0:T(4,128)S(1)} %add.194) | copy-start | bytes 2308
  38.3 9.0 copy-start.36
  47.2 34.4 %copy-start.16 = (bf16[1,2048,192]{1,2,0:T(8,128)(2,1)}, bf16[1,2048,192]{1,2,0:T(8,128)(2,1)S(1)}, u32[]{:S(2)}) copy-start(bf16[1,2048,192]{1,2,0:T(8,128)(2,1)S(1)} %all_gather.25) | copy-start | bytes 2359300
  71.2 10.5 %copy-start.29 = (f32[3,1024]{1,0:T(4,128)}, f32[3,1024]{1,0:T(4,128)S(1)}, u32[]{:S(2)}) copy-start(f32[3,1024]{1,0:T(4,128)S(1)} %get-tuple-element.135) | copy-start | bytes 36868
  81.6 10.6 %copy-start.39 = (f32[3,1024]{1,0:T(4,128)}, f32[3,1024]{1,0:T(4,128)S(1)}, u32[]{:S(2)}) copy-start(f32[3,1024]{1,0:T(4,128)S(1)} %fusion) | copy-start | bytes 36868
  92.3 2.3 copy-start.27
  94.6 246.3 %all-gather.8.cloned.1.call-start = ((), (), s32[]{:S(2)}) async-start(), calls=%async_computation.4 | async-start | bytes 1474560 | tf_op jit(solution)/shard_map/all_gather | solution.py:78
  95.3 371.7 %all-reduce.6.cloned.1.call-start = ((), (), s32[]{:S(2)}) async-start(), calls=%async_computation.5 | async-start | bytes 6291456 | tf_op jit(solution)/shard_map/psum | solution.py:124
  313.2 7.5 copy-start.49
  320.7 4.2 copy-start.12
  323.7 1.9 copy-start.3
  323.7 1.9 copy-start.40
  323.7 1.9 copy-start.50
  323.8 143.2 %copy-start.30 = (f32[1024]{0:T(1024)}, f32[1024]{0:T(1024)S(1)}, u32[]{:S(2)}) copy-start(f32[1024]{0:T(1024)S(1)} %broadcast_multiply_fusion.1) | copy-start | bytes 12292
  325.6 141.4 %copy-start.32 = (f32[1024]{0:T(1024)}, f32[1024]{0:T(1024)S(1)}, u32[]{:S(2)}) copy-start(f32[1024]{0:T(1024)S(1)} %fusion.58) | copy-start | bytes 12292
  327.3 2.8 copy-start.22
  330.1 2.7 copy-start.10
  345.7 121.3 %copy-start.51 = (f32[768]{0:T(1024)S(1)}, f32[768]{0:T(1024)}, u32[]{:S(2)}) copy-start(f32[768]{0:T(1024)} %param.21) | copy-start | bytes 9220
  345.8 260.5 %all-reduce.8.cloned.1.call-start = ((), (), s32[]{:S(2)}) async-start(), calls=%async_computation.6 | async-start | bytes 6291456 | tf_op jit(solution)/shard_map/psum | solution.py:139
  470.5 2.7 copy-start.54
  471.3 4.4 slice-start.3
  473.1 2.6 slice-start.4
  473.1 2.9 copy-start.15
  473.1 3.4 copy-start.56
  475.7 4.2 copy-start.7
  475.7 4.2 copy-start.44
  476.5 5.0 copy-start.18
  486.0 200.9 %reduce-scatter.4.cloned.1.call-start = ((), (), s32[]{:S(2)}) async-start(), calls=%async_computation.7 | async-start | bytes 2359296 | tf_op jit(solution)/shard_map/reduce_scatter | solution.py:175
  606.2 4.9 copy-start.43
  606.2 4.9 copy-start.31
  606.2 4.9 copy-start.33
  606.2 4.9 copy-start.41
  612.7 2.5 copy-start.17
  612.7 2.5 copy-start.37
  634.6 16.8 %copy-start.5 = (f32[1024,1,192]{0,2,1:T(8,128)S(1)}, f32[1024,1,192]{0,2,1:T(8,128)}, u32[]{:S(2)}) copy-start(f32[1024,1,192]{0,2,1:T(8,128)} %copy-done.4) | copy-start | bytes 2359300
  634.6 16.8 %copy-start.35 = (f32[3,64]{1,0:T(4,128)S(1)}, f32[3,64]{1,0:T(4,128)}, u32[]{:S(2)}) copy-start(f32[3,64]{1,0:T(4,128)} %copy-done.34) | copy-start | bytes 2308
  651.4 5.0 copy-start
  656.4 32.5 %reduce-scatter.6.cloned.1.call-start = ((), (), s32[]{:S(2)}) async-start(), calls=%async_computation.8 | async-start | bytes 2359296 | tf_op jit(solution)/shard_map/reduce_scatter | solution.py:178
  668.7 2.8 copy-start.8
  668.8 2.8 copy-start.45
  668.8 132.7 %reduce-scatter.8.cloned.1.call-start = ((), (), s32[]{:S(2)}) async-start(), calls=%async_computation.10 | async-start | bytes 11796480 | tf_op jit(solution)/shard_map/reduce_scatter | solution.py:189
  669.1 3.1 copy-start.26
  672.1 3.1 copy-start.23
  672.1 9.2 slice-start
  672.1 9.2 slice-start.1
  675.2 4.4 copy-start.2
  675.2 4.4 copy-start.28
  675.2 4.4 copy-start.38
  675.2 6.6 slice-start.2
  688.9 3.3 copy-start.13
  708.1 217.5 %all-reduce.10.cloned.1.call-start = ((), (), s32[]{:S(2)}) async-start(), calls=%async_computation.9 | async-start | bytes 6291456 | tf_op jit(solution)/shard_map/psum | solution.py:188
  712.8 241.1 %all-reduce.12.cloned.1.call-start = ((), (), s32[]{:S(2)}) async-start(), calls=%async_computation.11 | async-start | bytes 4718592 | tf_op jit(solution)/shard_map/psum | solution.py:203
  803.3 126.2 %copy-start.46 = (f32[768]{0:T(1024)S(1)}, f32[768]{0:T(1024)}, u32[]{:S(2)}) copy-start(f32[768]{0:T(1024)} %get-tuple-element.102) | copy-start | bytes 9220
  803.3 126.2 %copy-start.47 = (f32[768]{0:T(1024)S(1)}, f32[768]{0:T(1024)}, u32[]{:S(2)}) copy-start(f32[768]{0:T(1024)} %get-tuple-element.106) | copy-start | bytes 9220
  803.3 126.2 %copy-start.48 = (f32[768]{0:T(1024)S(1)}, f32[768]{0:T(1024)}, u32[]{:S(2)}) copy-start(f32[768]{0:T(1024)} %get-tuple-element.128) | copy-start | bytes 9220
  803.3 126.2 %copy-start.53 = (f32[768]{0:T(1024)S(1)}, f32[768]{0:T(1024)}, u32[]{:S(2)}) copy-start(f32[768]{0:T(1024)} %get-tuple-element.104) | copy-start | bytes 9220
  953.9 3.1 slice-start.6
  (10 other events, 13.0 us)
Sparse Core Ops, SparseCore 0:
  10.4 44.1 all-gather.5
  94.7 218.4 all-gather.9
  315.1 25.7 all-gather.7
  345.9 121.0 all-reduce.5
  486.1 120.0 all-reduce.7
  656.5 7.9 reduce-scatter.3
  668.9 8.1 reduce-scatter.5
  708.2 93.2 reduce-scatter.7
  804.4 121.0 all-reduce.9
  927.7 20.7 all-reduce.11
